TPU v7x, 32 devices: a whole 2x2x4 slice. The times are simulated.
32 devices in a mesh: groups: 2 (over x), row: 8 (over z, y), col: 2 (over core).
Axes of the slice: x: 2, y: 2, z: 4, core: 2. Of those that a mesh axis runs over, the one named last changes fastest.
Arguments:
- start_field: float32 [1024, 384, 256], P(('groups', 'row'), 'col'), parts along dimension 0, may hold values from 0 to 2
- counts: int32 [1024, 384, 256], P('groups', 'row', 'col'), parts along dimension 0, may hold values from -40 to 40
- weights: int32 [1024, 384, 256], P('groups', 'row', 'col'), parts along dimension 0, may hold values from 1 to 16
- strat_one: int32 [512, 512], replicated, may hold values from -64 to 63
- strat_two: int32 [384, 384], replicated, may hold values from -64 to 63
- strat_three: int32 [256, 256], replicated, may hold values from -64 to 63
Outputs:
- estimate: float32 [1024, 384, 256], P(('groups', 'row'), 'col'), parts along dimension 0
There are 2 independent parts, one for each index of `groups`. A program takes and returns all parts, laid end to end along the dimension named above; an argument that names none is the same for every part. Nothing has to cross between parts.
All inputs are finite; a program needn't handle non-finite values.
Results may differ from a plain program's by a relative error of at most 0.0001.
Values sent between devices are 32-bit elements; how exact they have to be, the bound alone decides.
No kernel may reach another device: no remote copies, remote signals or barrier semaphores. Data moves between devices by JAX's collectives and lax.ppermute only.
A program may use at most 128 MiB of HBM per device.

v0:
```python
import math

import jax
import jax.numpy as jnp
from jax import lax
from jax.sharding import PartitionSpec as P

highest = lax.Precision.HIGHEST
step_size = 0.5


def scaled(quant):
    order = quant.shape[0]
    return quant.astype(jnp.float32) * (1.0 / (37.0 * math.sqrt(order)))


def along_first(matrix, field):
    return jnp.einsum("ji,iab->jab", matrix, field, precision=highest)


def along_second(matrix, field):
    return jnp.einsum("ji,aib->ajb", matrix, field, precision=highest)


def along_third(matrix, field):
    return jnp.einsum("ji,abi->abj", matrix, field, precision=highest)


def pencil_forward(field, first, second, third):
    field = along_third(third, field)
    field = along_second(
        second, lax.all_to_all(field, "col", split_axis=2, concat_axis=1, tiled=True)
    )
    return along_first(first, lax.all_to_all(field, "row", split_axis=1, concat_axis=0, tiled=True))


def pencil_adjoint(field, first, second, third):
    field = along_first(first.T, field)
    field = along_second(
        second.T, lax.all_to_all(field, "row", split_axis=0, concat_axis=1, tiled=True)
    )
    return along_third(
        third.T, lax.all_to_all(field, "col", split_axis=1, concat_axis=2, tiled=True)
    )


def per_device(start_field, counts, weights, strat_one, strat_two, strat_three):
    first = scaled(strat_one)
    second = scaled(strat_two)
    third = scaled(strat_three)
    weight_field = weights.astype(jnp.float32) / 16.0
    target = counts.astype(jnp.float32) / 16.0
    estimate = start_field
    image = pencil_forward(estimate, first, second, third)
    residual = weight_field * (image - target)
    gradient = pencil_adjoint(residual, first, second, third)
    estimate = jnp.maximum(estimate - step_size * gradient, 0.0)
    return estimate


def solution(mesh):
    placed = (
        P(("groups", "row"), "col", None),
        P("groups", "row", "col"),
        P("groups", "row", "col"),
        P(),
        P(),
        P(),
    )
    return jax.shard_map(
        per_device,
        mesh=mesh,
        in_specs=placed,
        out_specs=P(("groups", "row"), "col", None),
        check_vma=False,
    )
```

profile of v0, /device:TPU:0, one launch (start us, length us, event | category | flops | bytes accessed | tf_op | source)
XLA Modules:
  0.0 937.4 jit_solution(8232785942097816457)
XLA Ops:
  0.0 14.9 %convolution_bitcast_fusion.2 = f32[64,192,256]{2,1,0:T(8,128)} fusion(f32[64,192,256]{2,1,0:T(8,128)} %param.6, s32[256,256]{1,0:T(8,128)} %param.11), kind=kOutput, calls=%fused_computation.13 | convolution fusion | flops 9663807488 | bytes 25427968 | tf_op jit(solution)/shard_map/ji,abi->abj/dot_general | solution.py:26
  14.9 17.4 %copy.37 = f32[64,192,256]{1,0,2:T(8,128)} copy(f32[64,192,256]{2,1,0:T(8,128)} %convolution_bitcast_fusion.2) | data formatting | bytes 25165824 | tf_op jit(solution)/shard_map/ji,abi->abj/dot_general | solution.py:26
  32.3 31.8 %all_to_all.72 = f32[64,192,256]{1,0,2:T(8,128)} all-to-all(f32[64,192,256]{1,0,2:T(8,128)} %copy.37), channel_id=1, replica_groups=mesh['groups'=2,'row'=8,'col'=2] {'col'}, dimensions={2} | all-to-all | bytes 25165824 | tf_op jit(solution)/shard_map/all_to_all | solution.py:32
  64.1 17.9 %copy.57 = f32[64,192,2,128]{3,2,1,0:T(2,128)} copy(f32[64,192,2,128]{1,0,3,2:T(8,128)} %bitcast.42) | data formatting | bytes 25165824 | tf_op jit(solution)/shard_map/all_to_all | solution.py:32
  82.1 0.0 copy-start.1
  82.1 11.0 %copy.39 = f32[64,2,192,128]{3,2,1,0:T(8,128)} copy(f32[64,2,192,128]{3,1,2,0:T(2,128)} %bitcast.44) | data formatting | bytes 25165824 | tf_op jit(solution)/shard_map/all_to_all | solution.py:32
  93.0 0.0 copy-done.1
  93.0 43.6 %convolution_bitcast_fusion.1 = f32[64,384,128]{1,2,0:T(8,128)} fusion(f32[64,384,128]{2,1,0:T(8,128)} %bitcast.40, s32[384,384]{1,0:T(8,128)S(1)} %copy-done.1), kind=kOutput, calls=%fused_computation.12 | convolution fusion | flops 14495809536 | bytes 25755648 | tf_op jit(solution)/shard_map/ji,aib->ajb/dot_general | solution.py:22
  136.6 12.7 %copy.41 = f32[64,384,128]{2,0,1:T(8,128)} copy(f32[64,384,128]{1,2,0:T(8,128)} %convolution_bitcast_fusion.1) | data formatting | bytes 25165824 | tf_op jit(solution)/shard_map/ji,aib->ajb/transpose | solution.py:22
  149.4 281.8 %all_to_all.73 = f32[64,384,128]{2,0,1:T(8,128)} all-to-all(f32[64,384,128]{2,0,1:T(8,128)} %copy.41), channel_id=1, replica_groups=mesh['groups'=2,'row'=8,'col'=2] {'row'}, dimensions={1} | all-to-all | bytes 25165824 | tf_op jit(solution)/shard_map/all_to_all | solution.py:34
  431.2 0.0 copy-start
  431.2 16.5 %copy.43 = f32[8,64,48,128]{3,2,1,0:T(8,128)} copy(f32[8,64,48,128]{3,1,2,0:T(8,128)} %bitcast.45) | data formatting | bytes 25165824 | tf_op jit(solution)/shard_map/all_to_all | solution.py:34
  447.7 0.0 copy-done
  447.7 28.6 %fusion.5 = f32[512,48,128]{2,0,1:T(8,128)S(1)} fusion(f32[512,48,128]{2,1,0:T(8,128)} %bitcast.43, s32[512,512]{1,0:T(8,128)S(1)} %copy-done), kind=kOutput, calls=%fused_computation.5 | convolution fusion | flops 19327877120 | bytes 26214400 | tf_op jit(solution)/shard_map/ji,iab->jab/dot_general | solution.py:18
  476.4 38.4 %fusion.3 = f32[512,48,128]{2,0,1:T(8,128)} fusion(f32[512,48,128]{2,0,1:T(8,128)S(1)} %fusion.5, s32[512,48,128]{2,1,0:T(8,128)} %param.7, s32[512,48,128]{2,1,0:T(8,128)} %param.8, s32[512,512]{1,0:T(8,128)S(1)} %copy-done), kind=kOutput, calls=%fused_computation.4 | convolution fusion | flops 19346751488 | bytes 51380224 | tf_op jit(solution)/shard_map/ji,iab->jab/dot_general | solution.py:18
  514.8 16.4 %copy.47 = f32[512,48,128]{2,1,0:T(8,128)} copy(f32[512,48,128]{2,0,1:T(8,128)} %fusion.3) | data formatting | bytes 25165824 | tf_op jit(solution)/shard_map/ji,iab->jab/dot_general | solution.py:18
  531.2 279.9 %all_to_all.74 = f32[512,48,128]{2,1,0:T(8,128)} all-to-all(f32[512,48,128]{2,1,0:T(8,128)} %copy.47), channel_id=1, replica_groups=mesh['groups'=2,'row'=8,'col'=2] {'row'}, dimensions={0} | all-to-all | bytes 25165824 | tf_op jit(solution)/shard_map/all_to_all | solution.py:40
  811.1 11.2 %copy.48 = f32[64,8,48,128]{3,2,1,0:T(8,128)} copy(f32[64,8,48,128]{3,2,0,1:T(8,128)} %bitcast.46) | data formatting | bytes 25165824 | tf_op jit(solution)/shard_map/all_to_all | solution.py:40
  822.3 27.5 %convolution_bitcast_fusion = f32[64,384,128]{1,2,0:T(8,128)} fusion(f32[64,384,128]{2,1,0:T(8,128)} %bitcast.41, s32[384,384]{1,0:T(8,128)S(1)} %copy-done.1), kind=kOutput, calls=%fused_computation.11 | convolution fusion | flops 14495809536 | bytes 25755648 | tf_op jit(solution)/shard_map/ji,aib->ajb/dot_general | solution.py:22
  849.8 12.6 %copy.50 = f32[64,384,128]{2,0,1:T(8,128)} copy(f32[64,384,128]{1,2,0:T(8,128)} %convolution_bitcast_fusion) | data formatting | bytes 25165824 | tf_op jit(solution)/shard_map/ji,aib->ajb/transpose | solution.py:22
  862.4 15.9 %all_to_all.75 = f32[64,384,128]{2,0,1:T(8,128)S(1)} all-to-all(f32[64,384,128]{2,0,1:T(8,128)} %copy.50), channel_id=1, replica_groups=mesh['groups'=2,'row'=8,'col'=2] {'col'}, dimensions={1} | all-to-all | bytes 25165824 | tf_op jit(solution)/shard_map/all_to_all | solution.py:43
  878.3 23.4 %copy.52 = f32[64,192,2,128]{3,2,1,0:T(2,128)} copy(f32[64,192,2,128]{3,0,1,2:T(8,128)S(1)} %bitcast.47) | data formatting | bytes 25165824 | tf_op jit(solution)/shard_map/all_to_all | solution.py:43
  901.7 0.0 copy-start.2
  901.7 16.6 %all_to_all.67 = f32[64,192,256]{2,1,0:T(8,128)} reshape(f32[64,192,2,128]{3,2,1,0:T(2,128)} %copy.52) | data formatting | bytes 25165824 | tf_op jit(solution)/shard_map/all_to_all | solution.py:43
  918.3 0.0 copy-done.2
  918.3 18.6 %subtract_maximum_fusion = f32[64,192,256]{2,1,0:T(8,128)} fusion(f32[64,192,256]{2,1,0:T(8,128)} %param.6, f32[64,192,256]{2,1,0:T(8,128)} %all_to_all.67, s32[256,256]{1,0:T(8,128)S(1)} %copy-done.2), kind=kOutput, calls=%fused_computation.9 | convolution fusion | flops 9673244672 | bytes 38010880 | tf_op jit(solution)/shard_map/ji,abi->abj/dot_general | solution.py:26
Async XLA Ops:
  82.1 11.0 %copy-start.1 = (s32[384,384]{1,0:T(8,128)S(1)}, s32[384,384]{1,0:T(8,128)}, u32[]{:S(2)}) copy-start(s32[384,384]{1,0:T(8,128)} %param.10) | copy-start | bytes 1769476
  431.2 16.5 %copy-start = (s32[512,512]{1,0:T(8,128)S(1)}, s32[512,512]{1,0:T(8,128)}, u32[]{:S(2)}) copy-start(s32[512,512]{1,0:T(8,128)} %param.9) | copy-start | bytes 3145732
  901.7 16.6 %copy-start.2 = (s32[256,256]{1,0:T(8,128)S(1)}, s32[256,256]{1,0:T(8,128)}, u32[]{:S(2)}) copy-start(s32[256,256]{1,0:T(8,128)} %param.11) | copy-start | bytes 786436
where the time goes:
time: 943 us; the launch traced here: 937 us
  blocking collectives  609 us (65%)
  matrix products  172 us (18%)
  local copies, waits for them, and re-layouts  156 us (17%)
    all_to_all x1, blocking collectives, pencil_forward(): lax.all_to_all(field, 'row', split_axis=1, concat_axis=0, tiled=True)  282 us
    all_to_all x1, blocking collectives, pencil_adjoint(): lax.all_to_all(field, 'row', split_axis=0, concat_axis=1, tiled=True)  280 us
    dot_general x2, matrix products, along_second(): return jnp.einsum('ji,aib->ajb', matrix, field, precision=highest)  71.1 us
    dot_general x2, matrix products, along_first(): return jnp.einsum('ji,iab->jab', matrix, field, precision=highest)  67 us
    all_to_all x2, local copies, waits for them, and re-layouts, pencil_adjoint(): lax.all_to_all(field, 'col', split_axis=1, concat_axis=2, tiled=True)  39.9 us
    dot_general x2, matrix products, along_third(): return jnp.einsum('ji,abi->abj', matrix, field, precision=highest)  33.5 us
    all_to_all x1, blocking collectives, pencil_forward(): lax.all_to_all(field, 'col', split_axis=2, concat_axis=1, tiled=True)  31.8 us
    all_to_all x2, local copies, waits for them, and re-layouts, pencil_forward(): lax.all_to_all(field, 'col', split_axis=2, concat_axis=1, tiled=True)  28.9 us

commit v1 on v0

v1 whole, which is shorter than its diff:
```python
import functools
import math

import jax
import jax.numpy as jnp
from jax import lax
from jax.experimental import pallas as pl
from jax.experimental.pallas import tpu as pltpu
from jax.sharding import PartitionSpec as P


highest = lax.Precision.HIGHEST
step_size = 0.5
f32 = jnp.float32
bf16 = jnp.bfloat16


def scale_of(order):
    return 1.0 / (37.0 * math.sqrt(order))


def scaled(quant):
    return quant.astype(f32) * scale_of(quant.shape[0])


def plain(start_field, counts, weights, strat_one, strat_two, strat_three):
    first, second, third = scaled(strat_one), scaled(strat_two), scaled(strat_three)
    field = jnp.einsum("ji,abi->abj", third, start_field, precision=highest)
    field = lax.all_to_all(field, "col", split_axis=2, concat_axis=1, tiled=True)
    field = jnp.einsum("ji,aib->ajb", second, field, precision=highest)
    field = lax.all_to_all(field, "row", split_axis=1, concat_axis=0, tiled=True)
    image = jnp.einsum("ji,iab->jab", first, field, precision=highest)
    field = weights.astype(f32) / 16.0 * (image - counts.astype(f32) / 16.0)
    field = jnp.einsum("ij,iab->jab", first, field, precision=highest)
    field = lax.all_to_all(field, "row", split_axis=0, concat_axis=1, tiled=True)
    field = jnp.einsum("ij,aib->ajb", second, field, precision=highest)
    field = lax.all_to_all(field, "col", split_axis=1, concat_axis=2, tiled=True)
    gradient = jnp.einsum("ij,abi->abj", third, field, precision=highest)
    return jnp.maximum(start_field - step_size * gradient, 0.0)


def halves(x):
    top = x.astype(bf16)
    return top, (x - top.astype(f32)).astype(bf16)


def mm(a, b):
    return jnp.dot(a, b, preferred_element_type=f32)


def at_start(body):
    pl.when(pl.program_id(0) == 0)(body)


def span(start, size):
    return pl.ds(pl.multiple_of(start, 8), size)


def third_kernel(x_ref, a_ref, own_ref, far_ref, w):
    ta, b, c = x_ref.shape
    ch = own_ref.shape[2]
    core = lax.axis_index("col")

    @at_start
    def _():
        rows = jnp.concatenate([a_ref[span(core * ch, ch), :], a_ref[span((1 - core) * ch, ch), :]], axis=0)
        t = rows.astype(f32).T.astype(bf16)
        w[:c, :] = t
        w[c:, :] = t

    hi, lo = halves(x_ref[...].reshape(ta * b, c))
    out = mm(jnp.concatenate([hi, lo], axis=1), w[...])
    own_ref[...] = out[:, :ch].reshape(ta, b, ch)
    far_ref[...] = out[:, ch:].reshape(ta, b, ch)


def second_kernel(bk, start, own_ref, far_ref, a_ref, *refs):
    outs, (wf, w) = refs[:-2], refs[-2:]
    ta, bl, lanes = own_ref.shape
    n2 = 2 * bl
    bh = outs[0].shape[1]
    r, core = lax.axis_index("row"), lax.axis_index("col")

    @at_start
    def _():
        for m in range(len(outs)):
            wf[m * bh : (m + 1) * bh, :] = a_ref[span((r ^ m) * bk + start, bh), :].astype(f32)
        t = wf[...].astype(bf16)
        w[:, :n2] = t
        w[:, n2:] = t

    for a in range(0, ta, 2):
        own, far = (jnp.concatenate([ref[a], ref[a + 1]], axis=1) for ref in (own_ref, far_ref))
        parts = [halves(jnp.where(core == c, own, far)) for c in range(2)]
        out = mm(w[...], jnp.concatenate([p[i] for i in range(2) for p in parts], axis=0))
        for m, o in enumerate(outs):
            o[a] = out[m * bh : (m + 1) * bh, :lanes]
            o[a + 1] = out[m * bh : (m + 1) * bh, lanes:]


def first_kernel(scale, rows, k_in, k_out, k_old, *refs):
    n_in, n_out = rows * k_in, rows * k_out
    pieces, (cnt_ref, wgt_ref, fwd_ref, bwd_ref) = refs[:n_in], refs[n_in : n_in + 4]
    outs = refs[n_in + 4 + k_old : n_in + 4 + k_old + n_out]
    field, res = refs[n_in + 4 + k_old + n_out :]
    n1, tb, c = cnt_ref.shape
    al = n1 // rows
    r = lax.axis_index("row")

    def flat(ref):
        return ref.reshape(ref.shape[0] * tb, c)

    def lines(ref, b):
        return flat(ref)[pl.ds(b, ref.shape[0], stride=tb), :]

    def places(some, k):
        for m in range(rows):
            at = (r ^ m) * al
            for ref in some[m * k : (m + 1) * k]:
                yield ref, span(at, ref.shape[0])
                at = at + ref.shape[0]

    def step(p, carry):
        for ref, at in places(pieces, k_in):
            for j in range(2):
                field[at, j * c : (j + 1) * c] = lines(ref, 2 * p + j)
        image = mm(fwd_ref[...], jnp.concatenate(halves(field[...]), axis=0))
        for j in range(2):
            wgt = lines(wgt_ref, 2 * p + j).astype(f32) * (1.0 / 16.0)
            tgt = lines(cnt_ref, 2 * p + j).astype(f32) * (1.0 / 16.0)
            hi, lo = halves(wgt * (image[:, j * c : (j + 1) * c] * scale - tgt))
            res[:n1, j * c : (j + 1) * c] = hi
            res[n1:, j * c : (j + 1) * c] = lo
        field[...] = mm(bwd_ref[...], res[...])
        for ref, at in places(outs, k_out):
            for j in range(2):
                flat(ref)[pl.ds(2 * p + j, ref.shape[0], stride=tb), :] = field[at, j * c : (j + 1) * c]
        return carry

    lax.fori_loop(0, tb // 2, step, 0)


def second_back_kernel(bk, places, *refs):
    pieces, (w_ref, own_ref, far_ref, x) = refs[:-4], refs[-4:]
    ta, bl, c = own_ref.shape
    r = lax.axis_index("row")

    def step(k, carry):
        a = 2 * k
        for (m, b0), p in zip(places, pieces):
            x[span((r ^ m) * bk + b0, p.shape[1]), :] = jnp.concatenate([p[a], p[a + 1]], axis=1)
        hi, lo = halves(x[...])
        out = mm(w_ref[...], jnp.concatenate([hi, lo], axis=0))
        for j in range(2):
            own_ref[a + j] = out[:bl, j * c : (j + 1) * c]
            far_ref[a + j] = out[bl:, j * c : (j + 1) * c]
        return carry

    lax.fori_loop(0, ta // 2, step, 0)


def third_back_kernel(scale, x_ref, own_ref, far_ref, w_ref, *rest):
    out_ref = rest[-1]
    ta, b, c = x_ref.shape
    ch = own_ref.shape[2]
    oh, ol = halves(own_ref[...].reshape(ta * b, ch))
    fh, fl = halves(far_ref[...].reshape(ta * b, ch))
    grad = mm(jnp.concatenate([oh, fh, ol, fl], axis=1), w_ref[...])
    out_ref[...] = jnp.maximum(x_ref[...] - (grad * scale).reshape(ta, b, c), 0.0)


def params(mib):
    return pltpu.CompilerParams(vmem_limit_bytes=mib * 2**20)


def cost(flops, nbytes):
    return pl.CostEstimate(flops=int(flops), bytes_accessed=int(nbytes), transcendentals=0)


def whole(array):
    return pl.BlockSpec(array.shape, lambda i: (0,) * array.ndim)


def tile_of(n, most):
    t = most
    while n % t:
        t //= 2
    return t


def pipelined(start_field, counts, weights, strat_one, strat_two, strat_three, rows, chunks, plan_f, plan_b, ranges):
    al, bl, n3 = start_field.shape
    n1, bk, ch = counts.shape
    n2 = strat_two.shape[0]
    bh = bk // 2
    core = lax.axis_index("col")
    scale = scale_of(n1) * scale_of(n2) * scale_of(n3)
    swap = [(0, 1), (1, 0)]

    def trade(pieces):
        sent = [pieces[0]]
        for m in range(1, rows):
            sent.append(lax.ppermute(pieces[m], "row", [(i, i ^ m) for i in range(rows)]))
        return sent

    def trade_cores(piece):
        return lax.ppermute(piece, "col", swap)

    def step_of(a0, na):
        return tile_of(math.gcd(na, a0) if a0 else na, min(4, na // 4))

    def third_part(a0, na):
        ta = step_of(a0, na)
        own, far = pl.pallas_call(
            third_kernel,
            grid=(na // ta,),
            in_specs=[pl.BlockSpec((ta, bl, n3), lambda i: (i + a0 // ta, 0, 0)), whole(strat_three)],
            out_specs=[pl.BlockSpec((ta, bl, ch), lambda i: (i, 0, 0))] * 2,
            out_shape=[jax.ShapeDtypeStruct((na, bl, ch), f32)] * 2,
            scratch_shapes=[pltpu.VMEM((2 * n3, n3), bf16)],
            compiler_params=params(54),
            cost_estimate=cost(4 * na * bl * n3 * n3, 8 * na * bl * n3),
            name="third",
        )(start_field, strat_three)
        return own, trade_cores(far)

    def second_part(b0, nb, c):
        (_, na), (own, far) = chunks[c], y[c]
        ta = step_of(0, na)
        spec = pl.BlockSpec((ta, bl, ch), lambda i: (i, 0, 0))
        pieces = pl.pallas_call(
            functools.partial(second_kernel, bk, b0),
            grid=(na // ta,),
            in_specs=[spec, spec, whole(strat_two)],
            out_specs=[pl.BlockSpec((ta, nb, ch), lambda i: (i, 0, 0))] * rows,
            out_shape=[jax.ShapeDtypeStruct((na, nb, ch), f32)] * rows,
            scratch_shapes=[
                pltpu.VMEM((rows * nb, n2), f32),
                pltpu.VMEM((rows * nb, 2 * n2), bf16),
            ],
            compiler_params=params(48),
            cost_estimate=cost(4 * na * nb * rows * n2 * ch, 4 * na * ch * (n2 + nb * rows)),
            name="second",
        )(own, far, strat_two)
        return trade(pieces)

    y = [third_part(a0, na) for a0, na in chunks]
    got_f = [second_part(*part) for part in plan_f]

    late = lax.optimization_barrier((strat_one, strat_two, strat_three, got_f[0][0]))
    first = late[0].astype(bf16)
    first_f = jnp.concatenate([first, first], axis=1)
    first_b = jnp.concatenate([first.T, first.T], axis=1)

    def own_first(a, axis):
        n = a.shape[axis] // 2
        return jnp.concatenate(
            [lax.dynamic_slice_in_dim(a, core * n, n, axis), lax.dynamic_slice_in_dim(a, (1 - core) * n, n, axis)],
            axis,
        )

    second_t = own_first(late[1].astype(bf16), 1).T
    second_b = jnp.concatenate([second_t, second_t], axis=1)
    third = own_first(late[2].astype(bf16), 0)
    third_b = jnp.concatenate([third, third], axis=0)

    made = {}

    def first_part(h):
        pieces, specs = [], []
        for m in range(rows):
            for c, (_, na) in enumerate(chunks):
                (k, b0) = next((k, b) for k, (b, n, e) in enumerate(plan_f) if e == c and b <= h * bh < b + n)
                pieces.append(got_f[k][m])
                specs.append(pl.BlockSpec((na, 8, ch), lambda i, o=(h * bh - b0) // 8: (0, i + o, 0)))
        sets = sorted((a0, k) for k, (a0, _, b0, nb) in enumerate(plan_b) if b0 <= h * bh < b0 + nb)
        keys = [(k, m) for m in range(rows) for _, k in sets]
        old = [key for key in keys if key in made]
        out_specs, out_shape = [], []
        for k, _ in keys:
            _, na, b0, nb = plan_b[k]
            out_specs.append(pl.BlockSpec((na, 8, ch), lambda i, o=(h * bh - b0) // 8: (0, i + o, 0)))
            out_shape.append(jax.ShapeDtypeStruct((na, nb, ch), f32))
        side = pl.BlockSpec((n1, 8, ch), lambda i: (0, i + h * bh // 8, 0))
        outs = pl.pallas_call(
            functools.partial(first_kernel, scale, rows, len(chunks), len(sets), len(old)),
            grid=(bh // 8,),
            in_specs=specs
            + [side, side, whole(first_f), whole(first_b)]
            + [pl.BlockSpec(memory_space=pl.ANY)] * len(old),
            out_specs=out_specs,
            out_shape=out_shape,
            input_output_aliases={len(pieces) + 4 + i: keys.index(key) for i, key in enumerate(old)},
            scratch_shapes=[pltpu.VMEM((n1, 2 * ch), f32), pltpu.VMEM((2 * n1, 2 * ch), bf16)],
            compiler_params=params(60),
            cost_estimate=cost(8 * n1 * n1 * bh * ch, 16 * n1 * bh * ch),
            name="first",
        )(*pieces, counts, weights, first_f, first_b, *[made[key] for key in old])
        made.update(zip(keys, outs))

    first_part(0)
    first_part(1)
    got_b = [trade([made[k, m] for m in range(rows)]) for k in range(len(plan_b))]

    last = min(a0 for a0, na in ranges if na * bl * n3 <= 2**20)
    near = lax.slice_in_dim(start_field, last, al)

    out = None
    for a0, na in ranges:
        pieces, places, specs = [], [], []
        ta = step_of(a0, na)
        for k, (s0, n, b0, nb) in enumerate(plan_b):
            if s0 <= a0 and a0 + na <= s0 + n:
                for m in range(rows):
                    pieces.append(got_b[k][m])
                    places.append((m, b0))
                    specs.append(pl.BlockSpec((ta, nb, ch), lambda i, o=(a0 - s0) // ta: (i + o, 0, 0)))
        half = pl.BlockSpec((ta, bl, ch), lambda i: (i, 0, 0))
        own, far = pl.pallas_call(
            functools.partial(second_back_kernel, bk, places),
            grid=(na // ta,),
            in_specs=specs + [whole(second_b)],
            out_specs=[half] * 2,
            out_shape=[jax.ShapeDtypeStruct((na, bl, ch), f32)] * 2,
            scratch_shapes=[pltpu.VMEM((n2, 2 * ch), f32)],
            compiler_params=params(48),
            cost_estimate=cost(4 * na * n2 * n2 * ch, 8 * na * n2 * ch),
            name="second_back",
        )(*pieces, second_b)
        far = trade_cores(far)
        full = pl.BlockSpec((ta, bl, n3), lambda i, o=a0 // ta: (i + o, 0, 0))
        extra = [] if out is None else [out]
        x = start_field
        x_spec = full
        if a0 >= last:
            x_spec = pl.BlockSpec((ta, bl, n3), lambda i, o=(a0 - last) // ta: (i + o, 0, 0))
            x, own, far = (pltpu.with_memory_space_constraint(v, pltpu.VMEM) for v in (near, own, far))
        out = pl.pallas_call(
            functools.partial(third_back_kernel, step_size * scale),
            grid=(na // ta,),
            in_specs=[x_spec, half, half, whole(third_b)] + [pl.BlockSpec(memory_space=pl.ANY)] * len(extra),
            out_specs=full,
            out_shape=jax.ShapeDtypeStruct(start_field.shape, f32),
            input_output_aliases={4: 0} if extra else {},
            compiler_params=params(54),
            cost_estimate=cost(4 * na * bl * n3 * n3, 12 * na * bl * n3),
            name="third_back",
        )(x, own, far, third_b, *extra)
    return out


def plans(al, bk):
    e, bh = al // 8, bk // 2
    chunks = [(0, e), (e, 3 * e), (4 * e, 4 * e)]
    plan_f = [(0, bk, 0), (0, bh, 1), (0, bh, 2), (bh, bh, 1), (bh, bh, 2)]
    plan_b = [
        (0, 6 * e, 0, bh), (0, 3 * e, bh, bh), (3 * e, 3 * e, bh, bh), (6 * e, e, 0, bk), (7 * e, e, 0, bk),
    ]
    ranges = [(0, 3 * e), (3 * e, 3 * e), (6 * e, e), (7 * e, e)]
    return chunks, plan_f, plan_b, ranges


def per_device(rows, cols, *args):
    al, bl, _ = args[0].shape
    _, bk, ch = args[1].shape
    fits = cols == 2 and rows & (rows - 1) == 0 and 1 < rows <= 16 and al % 64 == 0 and bk % 16 == 0
    if not (fits and bl % 16 == 0 and ch % 128 == 0):
        return plain(*args)
    return pipelined(*args, rows, *plans(al, bk))


def solution(mesh):
    placed = (
        P(("groups", "row"), "col", None),
        P("groups", "row", "col"),
        P("groups", "row", "col"),
        P(),
        P(),
        P(),
    )
    return jax.shard_map(
        functools.partial(per_device, mesh.shape["row"], mesh.shape["col"]),
        mesh=mesh,
        in_specs=placed,
        out_specs=P(("groups", "row"), "col", None),
        check_vma=False,
    )
```

time: 943 us -> 676 us (0.72)
  blocking collectives: 609 us -> 0 us
  waiting for transfers between devices: 0 us -> 341 us
  matrix products: 172 us -> 0 us
  starting transfers between devices: 0 us -> 162 us
  Pallas kernels: 0 us -> 141 us
  local copies, waits for them, and re-layouts: 156 us -> 21.5 us
    all_to_all x4 -> x0, blocking collectives: 609 us -> none  [the longest x1 282 us: pencil_forward(): lax.all_to_all(field, 'row', split_axis=1, concat_axis=0, tiled=True)]
    ppermute x0 -> x77, waiting for transfers between devices: none -> 341 us  [the longest x70 339 us: trade(): lax.ppermute(pieces[m], 'row', [(i, i ^ m) for i in range(rows)])]
    dot_general x6 -> x0, matrix products: 172 us -> none  [the longest x2 71.1 us: along_second(): return jnp.einsum('ji,aib->ajb', matrix, field, precision=highest)]
    ppermute x0 -> x77, starting transfers between devices: none -> 162 us  [the longest x70 161 us: trade(): lax.ppermute(pieces[m], 'row', [(i, i ^ m) for i in range(rows)])]
    pallas_call x0 -> x18, Pallas kernels: none -> 141 us  [the longest x2 49.7 us: first_part(): pl.pallas_call(functools.partial(first_kernel, scale, rows, len(chunks),...]
    all_to_all x6 -> x0, local copies, waits for them, and re-layouts: 96.6 us -> none  [the longest x2 39.9 us: pencil_adjoint(): lax.all_to_all(field, 'col', split_axis=1, concat_axis=2, tiled=True)]
    dot_general x2 -> x0, local copies, waits for them, and re-layouts: 33.9 us -> none  [the longest x1 17.4 us: along_third(): return jnp.einsum('ji,abi->abj', matrix, field, precision=highest)]
    transpose x2 -> x0, local copies, waits for them, and re-layouts: 25.4 us -> none  [along_second(): return jnp.einsum('ji,aib->ajb', matrix, field, precision=highest)]
  transfers between devices with their start and end apart: 0 -> 77, of which waited for: 0 -> 29; matrix products, arithmetic and copies ran while one was open for 0% -> 2% of each run, Pallas kernels for 0% -> 16%
where the time goes in v1:
time: 676 us; the launch traced here: 671 us
  waiting for transfers between devices  341 us (50%)
  starting transfers between devices  162 us (24%)
  Pallas kernels  141 us (21%)
  local copies, waits for them, and re-layouts  21.5 us (3%)
    ppermute x70, waiting for transfers between devices, trade(): lax.ppermute(pieces[m], 'row', [(i, i ^ m) for i in range(rows)])  339 us
    ppermute x70, starting transfers between devices, trade(): lax.ppermute(pieces[m], 'row', [(i, i ^ m) for i in range(rows)])  161 us
    pallas_call x2, Pallas kernels, first_part(): pl.pallas_call(functools.partial(first_kernel, scale, rows, len(chunks),...  49.7 us
    pallas_call x5, Pallas kernels, second_part(): pl.pallas_call(functools.partial(second_kernel, bk, b0), grid=(na // ta,)...  26 us
    pallas_call x4, Pallas kernels, pipelined(): pl.pallas_call(functools.partial(third_back_kernel, step_size * scale), g...  24.2 us
    pallas_call x3, Pallas kernels, third_part(): pl.pallas_call(third_kernel, grid=(na // ta,), in_specs=[pl.BlockSpec((ta...  20.9 us
    pallas_call x4, Pallas kernels, pipelined(): pl.pallas_call(functools.partial(second_back_kernel, bk, places), grid=(n...  19.6 us
    unnamed x166, local copies, waits for them, and re-layouts  14.3 us
  transfers between devices with their start and end apart: 77, of which 29 were waited for; matrix products, arithmetic and copies ran while one was open for 2% of the time, Pallas kernels for 16%

profile of v1, /device:TPU:0, one launch (start us, length us, event | category | flops | bytes accessed | tf_op | source)
XLA Modules:
  0.0 671.4 jit_solution(3137805390725886078)
XLA Ops:
  0.0 7.2 %third.4 = (f32[24,192,128]{2,1,0:T(8,128)}, f32[24,192,128]{2,1,0:T(8,128)}) custom-call(f32[64,192,256]{2,1,0:T(8,128)} %x_ref.9, s32[256,256]{1,0:T(8,128)} %a_ref.12), custom_call_target="tpu_custom_call" | custom-call | flops 1207959552 | bytes 9437184 | tf_op jit(solution)/shard_map/third/pallas_call | solution.py:214
  7.7 9.3 %third.5 = (f32[32,192,128]{2,1,0:T(8,128)}, f32[32,192,128]{2,1,0:T(8,128)}) custom-call(f32[64,192,256]{2,1,0:T(8,128)} %x_ref.9, s32[256,256]{1,0:T(8,128)} %a_ref.12), custom_call_target="tpu_custom_call" | custom-call | flops 1610612736 | bytes 12582912 | tf_op jit(solution)/shard_map/third/pallas_call | solution.py:214
  17.0 4.5 third.3
  26.7 4.0 collective-permute-start.12
  35.6 13.5 %collective-permute-done.12.refs_12_ = f32[8,48,128]{2,1,0:T(8,128)S(1)} collective-permute-done((f32[8,48,128]{2,1,0:T(8,128)S(1)}, f32[8,48,128]{2,1,0:T(8,128)S(1)}, u32[]{:S(2)}, u32[]{:S(2)}) %collective-permute-start.12) | collective-permute-done | bytes 196640 | tf_op jit(solution)/shard_map/ppermute | solution.py:203
  49.1 4.0 collective-permute-start.21
  53.1 5.7 collective-permute-done.15.refs_15_
  63.7 4.7 second.8
  76.8 5.4 second.6
  83.6 6.3 collective-permute-done.26.refs_7_
  97.6 21.6 %collective-permute-done.32.refs_16_ = f32[24,24,128]{2,1,0:T(8,128)S(1)} collective-permute-done((f32[24,24,128]{2,1,0:T(8,128)S(1)}, f32[24,24,128]{2,1,0:T(8,128)S(1)}, u32[]{:S(2)}, u32[]{:S(2)}) %collective-permute-start.32) | collective-permute-done | bytes 294944 | tf_op jit(solution)/shard_map/ppermute | solution.py:203
  119.3 11.6 %collective-permute-start.16 = (f32[24,24,128]{2,1,0:T(8,128)S(1)}, f32[24,24,128]{2,1,0:T(8,128)S(1)}, u32[]{:S(2)}, u32[]{:S(2)}) collective-permute-start(f32[24,24,128]{2,1,0:T(8,128)S(1)} %get-tuple-element.140), channel_id=1, source_target_pairs={{0,10},{2,8},{4,14},{6,12},{8,2},{10,0},{12,6},{14,4},{1,11},{3,9}... | collective-permute-start | bytes 884744 | tf_op jit(solution)/shard_map/ppermute | solution.py:203
  136.3 7.6 %second.9 = (f32[32,24,128]{2,1,0:T(8,128)S(1)}, f32[32,24,128]{2,1,0:T(8,128)}, f32[32,24,128]{2,1,0:T(8,128)}, f32[32,24,128]{2,1,0:T(8,128)}, f32[32,24,128]{...) custom-call(f32[32,192,128]{2,1,0:T(8,128)} %get-tuple-element.124.own_ref, ...), custom_call_target="tpu_custom_call" | custom-call | flops 1207959552 | bytes 9437184 | tf_op jit(solution)/shard_map/second/pallas_call | solution.py:231
  144.7 17.2 %collective-permute-done.13.refs_13_ = f32[24,24,128]{2,1,0:T(8,128)S(1)} collective-permute-done((f32[24,24,128]{2,1,0:T(8,128)S(1)}, f32[24,24,128]{2,1,0:T(8,128)S(1)}, u32[]{:S(2)}, u32[]{:S(2)}) %collective-permute-start.13) | collective-permute-done | bytes 294944 | tf_op jit(solution)/shard_map/ppermute | solution.py:203
  163.5 5.8 collective-permute-done.16.refs_16_
  170.7 5.4 collective-permute-start.29
  176.1 7.4 %collective-permute-start.31 = (f32[32,24,128]{2,1,0:T(8,128)}, f32[32,24,128]{2,1,0:T(8,128)}, u32[]{:S(2)}, u32[]{:S(2)}) collective-permute-start(f32[32,24,128]{2,1,0:T(8,128)} %get-tuple-element.158), channel_id=1, source_target_pairs={{0,8},{2,10},{4,12},{6,14},{8,0},{10,2},{12,4},{14,6},{1,9},{3,11}... | collective-permute-start | bytes 1179656 | tf_op jit(solution)/shard_map/ppermute | solution.py:203
  189.9 6.8 %second.7 = (f32[32,24,128]{2,1,0:T(8,128)S(1)}, f32[32,24,128]{2,1,0:T(8,128)S(1)}, f32[32,24,128]{2,1,0:T(8,128)S(1)}, f32[32,24,128]{2,1,0:T(8,128)S(1)}, f32...) custom-call(f32[32,192,128]{2,1,0:T(8,128)} %get-tuple-element.124.o, ...), custom_call_target="tpu_custom_call" | custom-call | flops 1207959552 | bytes 9437184 | tf_op jit(solution)/shard_map/second/pallas_call | solution.py:231
  212.6 50.0 %collective-permute-done.33.refs_17_ = f32[32,24,128]{2,1,0:T(8,128)S(1)} collective-permute-done((f32[32,24,128]{2,1,0:T(8,128)S(1)}, f32[32,24,128]{2,1,0:T(8,128)S(1)}, u32[]{:S(2)}, u32[]{:S(2)}) %collective-permute-start.33) | collective-permute-done | bytes 393248 | tf_op jit(solution)/shard_map/ppermute | solution.py:203
  262.7 4.5 collective-permute-start.23
  268.0 28.2 %collective-permute-done.14.refs_14_ = f32[32,24,128]{2,1,0:T(8,128)S(1)} collective-permute-done((f32[32,24,128]{2,1,0:T(8,128)S(1)}, f32[32,24,128]{2,1,0:T(8,128)S(1)}, u32[]{:S(2)}, u32[]{:S(2)}) %collective-permute-start.14) | collective-permute-done | bytes 393248 | tf_op jit(solution)/shard_map/ppermute | solution.py:203
  297.0 24.9 %first.2 = (f32[48,24,128]{2,1,0:T(8,128)}, f32[8,48,128]{2,1,0:T(8,128)}, f32[8,48,128]{2,1,0:T(8,128)}, f32[48,24,128]{2,1,0:T(8,128)}, f32[8,48,128]{2,1,0:T(...) custom-call(f32[8,48,128]{2,1,0:T(8,128)} %copy-done.4, ...), custom_call_target="tpu_custom_call" | custom-call | flops 6442450944 | bytes 25165824 | tf_op jit(solution)/shard_map/first/pallas_call | solution.py:285
  322.9 24.9 %first.3 = (f32[24,24,128]{2,1,0:T(8,128)}, f32[24,24,128]{2,1,0:T(8,128)}, f32[8,48,128]{2,1,0:T(8,128)}, f32[8,48,128]{2,1,0:T(8,128)}, f32[24,24,128]{2,1,0:T...) custom-call(f32[8,48,128]{2,1,0:T(8,128)} %copy-done.4, ...), custom_call_target="tpu_custom_call", output_to_operand_aliasing={{2}: (28, {}), {3}: (29, {}), {6}: (30, {}), {7}: (31, {}),... | custom-call | flops 6442450944 | bytes 25165824 | tf_op jit(solution)/shard_map/first/pallas_call | solution.py:285
  361.0 5.0 collective-permute-done.70.refs_10_
  372.3 4.5 collective-permute-done.72.refs_12_
  379.6 8.1 %collective-permute-done.73.refs_13_ = f32[24,24,128]{2,1,0:T(8,128)S(1)} collective-permute-done((f32[24,24,128]{2,1,0:T(8,128)}, f32[24,24,128]{2,1,0:T(8,128)S(1)}, u32[]{:S(2)}, u32[]{:S(2)}) %collective-permute-start.73) | collective-permute-done | bytes 294944 | tf_op jit(solution)/shard_map/ppermute | solution.py:203
  390.4 5.9 collective-permute-start.62
  396.3 9.1 %collective-permute-done.75.refs_15_ = f32[24,24,128]{2,1,0:T(8,128)S(1)} collective-permute-done((f32[24,24,128]{2,1,0:T(8,128)}, f32[24,24,128]{2,1,0:T(8,128)S(1)}, u32[]{:S(2)}, u32[]{:S(2)}) %collective-permute-start.75) | collective-permute-done | bytes 294944 | tf_op jit(solution)/shard_map/ppermute | solution.py:203
  409.0 8.7 %collective-permute-done.62.refs_10_ = f32[24,24,128]{2,1,0:T(8,128)S(1)} collective-permute-done((f32[24,24,128]{2,1,0:T(8,128)}, f32[24,24,128]{2,1,0:T(8,128)S(1)}, u32[]{:S(2)}, u32[]{:S(2)}) %collective-permute-start.62) | collective-permute-done | bytes 294944 | tf_op jit(solution)/shard_map/ppermute | solution.py:203
  418.5 8.7 %collective-permute-start.59 = (f32[48,24,128]{2,1,0:T(8,128)}, f32[48,24,128]{2,1,0:T(8,128)}, u32[]{:S(2)}, u32[]{:S(2)}) collective-permute-start(f32[48,24,128]{2,1,0:T(8,128)} %get-tuple-element.209), channel_id=1, source_target_pairs={{0,12},{2,14},{4,8},{6,10},{8,4},{10,6},{12,0},{14,2},{1,13},{3,15... | collective-permute-start | bytes 1769480 | tf_op jit(solution)/shard_map/ppermute | solution.py:203
  433.8 33.3 %collective-permute-done.57.refs_4_ = f32[48,24,128]{2,1,0:T(8,128)S(1)} collective-permute-done((f32[48,24,128]{2,1,0:T(8,128)}, f32[48,24,128]{2,1,0:T(8,128)S(1)}, u32[]{:S(2)}, u32[]{:S(2)}) %collective-permute-start.57) | collective-permute-done | bytes 589856 | tf_op jit(solution)/shard_map/ppermute | solution.py:203
  467.2 36.2 %collective-permute-done.58.refs_5_ = f32[48,24,128]{2,1,0:T(8,128)} collective-permute-done((f32[48,24,128]{2,1,0:T(8,128)}, f32[48,24,128]{2,1,0:T(8,128)}, u32[]{:S(2)}, u32[]{:S(2)}) %collective-permute-start.58) | collective-permute-done | bytes 589856 | tf_op jit(solution)/shard_map/ppermute | solution.py:203
  506.8 7.3 %second_back.7 = (f32[24,192,128]{2,1,0:T(8,128)}, f32[24,192,128]{2,1,0:T(8,128)}) custom-call(f32[48,24,128]{2,1,0:T(8,128)S(1)} %copy-done.3, f32[48,24,128]{2,1,0:T(8,128)S(1)} %collective-permute-done.54.refs_1_, f32[48,24,128]{2,1,0:T(8,128)S(1)} %collective-permute-done.55.refs_2_, f32[48,24,128]{2,1,0:T(8,128)S(1)} %collective-permute-done.56.refs_3_, ...), custom_call_target="tpu_custom_call" | custom-call | flops 1811939328 | bytes 9437184 | tf_op jit(solution)/shard_map/second_back/pallas_call | solution.py:319
  514.1 25.9 %collective-permute-done.64.refs_12_ = f32[24,24,128]{2,1,0:T(8,128)S(1)} collective-permute-done((f32[24,24,128]{2,1,0:T(8,128)}, f32[24,24,128]{2,1,0:T(8,128)S(1)}, u32[]{:S(2)}, u32[]{:S(2)}) %collective-permute-start.64) | collective-permute-done | bytes 294944 | tf_op jit(solution)/shard_map/ppermute | solution.py:203
  540.0 8.4 %collective-permute-done.65.refs_13_ = f32[24,24,128]{2,1,0:T(8,128)S(1)} collective-permute-done((f32[24,24,128]{2,1,0:T(8,128)}, f32[24,24,128]{2,1,0:T(8,128)S(1)}, u32[]{:S(2)}, u32[]{:S(2)}) %collective-permute-start.65) | collective-permute-done | bytes 294944 | tf_op jit(solution)/shard_map/ppermute | solution.py:203
  548.6 7.4 %second_back.6 = (f32[24,192,128]{2,1,0:T(8,128)}, f32[24,192,128]{2,1,0:T(8,128)}) custom-call(f32[48,24,128]{2,1,0:T(8,128)S(1)} %copy-done.3, f32[48,24,128]{2,1,0:T(8,128)S(1)} %collective-permute-done.54.refs_1_, f32[48,24,128]{2,1,0:T(8,128)S(1)} %collective-permute-done.55.refs_2_, f32[48,24,128]{2,1,0:T(8,128)S(1)} %collective-permute-done.56.refs_3_, ...), custom_call_target="tpu_custom_call" | custom-call | flops 1811939328 | bytes 9437184 | tf_op jit(solution)/shard_map/second_back/pallas_call | solution.py:319
  556.1 10.6 %collective-permute-start.47 = (f32[8,48,128]{2,1,0:T(8,128)S(1)}, f32[8,48,128]{2,1,0:T(8,128)S(1)}, u32[]{:S(2)}, u32[]{:S(2)}) collective-permute-start(f32[8,48,128]{2,1,0:T(8,128)S(1)} %copy-done.71), channel_id=1, source_target_pairs={{0,4},{2,6},{4,0},{6,2},{8,12},{10,14},{12,8},{14,10},{1,5},{3,7},... | collective-permute-start | bytes 589832 | tf_op jit(solution)/shard_map/ppermute | solution.py:203
  566.7 6.9 %collective-permute-start.49 = (f32[8,48,128]{2,1,0:T(8,128)S(1)}, f32[8,48,128]{2,1,0:T(8,128)S(1)}, u32[]{:S(2)}, u32[]{:S(2)}) collective-permute-start(f32[8,48,128]{2,1,0:T(8,128)S(1)} %copy-done.75), channel_id=1, source_target_pairs={{0,8},{2,10},{4,12},{6,14},{8,0},{10,2},{12,4},{14,6},{1,9},{3,11}... | collective-permute-start | bytes 589832 | tf_op jit(solution)/shard_map/ppermute | solution.py:203
  575.6 4.7 collective-permute-done.48.refs_3_
  582.1 12.0 %collective-permute-done.49.refs_4_ = f32[8,48,128]{2,1,0:T(8,128)S(1)} collective-permute-done((f32[8,48,128]{2,1,0:T(8,128)S(1)}, f32[8,48,128]{2,1,0:T(8,128)S(1)}, u32[]{:S(2)}, u32[]{:S(2)}) %collective-permute-start.49) | collective-permute-done | bytes 196640 | tf_op jit(solution)/shard_map/ppermute | solution.py:203
  599.8 5.4 collective-permute-start.39
  605.3 4.0 collective-permute-start.40
  612.2 4.2 collective-permute-done.40.refs_3_
  618.5 13.8 %collective-permute-done.41.refs_4_ = f32[8,48,128]{2,1,0:T(8,128)S(1)} collective-permute-done((f32[8,48,128]{2,1,0:T(8,128)S(1)}, f32[8,48,128]{2,1,0:T(8,128)S(1)}, u32[]{:S(2)}, u32[]{:S(2)}) %collective-permute-start.41) | collective-permute-done | bytes 196640 | tf_op jit(solution)/shard_map/ppermute | solution.py:203
  647.1 8.0 %third_back.4.rest_0_ = f32[64,192,256]{2,1,0:T(8,128)} custom-call(f32[64,192,256]{2,1,0:T(8,128)} %x_ref.9, f32[24,192,128]{2,1,0:T(8,128)} %get-tuple-element.229.own_ref, f32[24,192,128]{2,1,0:T(8,128)} %collective-permute-done.76.far_ref, bf16[512,256]{1,0:T(8,128)(2,1)} %pad_maximum_fusion.3.w_ref), custom_call_target="tpu_custom_call" | custom-call | flops 1207959552 | bytes 14155776 | tf_op jit(solution)/shard_map/third_back/pallas_call | solution.py:338
  655.1 8.1 %third_back.5.rest_0_ = f32[64,192,256]{2,1,0:T(8,128)} custom-call(f32[64,192,256]{2,1,0:T(8,128)} %x_ref.9, f32[24,192,128]{2,1,0:T(8,128)} %get-tuple-element.219.own_ref, f32[24,192,128]{2,1,0:T(8,128)} %collective-permute-done.68.far_ref, bf16[512,256]{1,0:T(8,128)(2,1)} %pad_maximum_fusion.3.w_ref, ...), custom_call_target="tpu_custom_call", output_to_operand_aliasing={{}: (4, {})} | custom-call | flops 1207959552 | bytes 14155776 | tf_op jit(solution)/shard_map/third_back/pallas_call | solution.py:338
  663.2 4.1 third_back.6.rest_0_
  667.3 4.1 third_back.7
  (305 shorter events, 135.6 us)
Async XLA Ops:
  7.2 55.1 %collective-permute-start.1 = (f32[24,192,128]{2,1,0:T(8,128)}, f32[24,192,128]{2,1,0:T(8,128)S(1)}, u32[]{:S(2)}, u32[]{:S(2)}) collective-permute-start(f32[24,192,128]{2,1,0:T(8,128)} %get-tuple-element.122), channel_id=1, source_target_pairs={{0,1},{1,0},{2,3},{3,2},{4,5},{5,4},{6,7},{7,6},{8,9},{9,8},{10,11... | collective-permute-start | bytes 7077896 | tf_op jit(solution)/shard_map/ppermute | solution.py:207
  17.0 117.6 %collective-permute-start.2 = (f32[32,192,128]{2,1,0:T(8,128)}, f32[32,192,128]{2,1,0:T(8,128)S(1)}, u32[]{:S(2)}, u32[]{:S(2)}) collective-permute-start(f32[32,192,128]{2,1,0:T(8,128)} %get-tuple-element.125), channel_id=1, source_target_pairs={{0,1},{1,0},{2,3},{3,2},{4,5},{5,4},{6,7},{7,6},{8,9},{9,8},{10,11... | collective-permute-start | bytes 9437192 | tf_op jit(solution)/shard_map/ppermute | solution.py:207
  30.7 28.1 %collective-permute-start.15 = (f32[8,48,128]{2,1,0:T(8,128)S(1)}, f32[8,48,128]{2,1,0:T(8,128)S(1)}, u32[]{:S(2)}, u32[]{:S(2)}) collective-permute-start(f32[8,48,128]{2,1,0:T(8,128)S(1)} %get-tuple-element.139), channel_id=1, source_target_pairs={{0,10},{2,8},{4,14},{6,12},{8,2},{10,0},{12,6},{14,4},{1,11},{3,9}... | collective-permute-start | bytes 589832 | tf_op jit(solution)/shard_map/ppermute | solution.py:203
  32.0 26.8 %collective-permute-start.18 = (f32[8,48,128]{2,1,0:T(8,128)S(1)}, f32[8,48,128]{2,1,0:T(8,128)S(1)}, u32[]{:S(2)}, u32[]{:S(2)}) collective-permute-start(f32[8,48,128]{2,1,0:T(8,128)S(1)} %get-tuple-element.142), channel_id=1, source_target_pairs={{0,12},{2,14},{4,8},{6,10},{8,4},{10,6},{12,0},{14,2},{1,13},{3,15... | collective-permute-start | bytes 589832 | tf_op jit(solution)/shard_map/ppermute | solution.py:203
  82.3 37.0 %collective-permute-start.32 = (f32[24,24,128]{2,1,0:T(8,128)S(1)}, f32[24,24,128]{2,1,0:T(8,128)S(1)}, u32[]{:S(2)}, u32[]{:S(2)}) collective-permute-start(f32[24,24,128]{2,1,0:T(8,128)S(1)} %get-tuple-element.159), channel_id=1, source_target_pairs={{0,10},{2,8},{4,14},{6,12},{8,2},{10,0},{12,6},{14,4},{1,11},{3,9}... | collective-permute-start | bytes 884744 | tf_op jit(solution)/shard_map/ppermute | solution.py:203
  90.0 29.3 %collective-permute-start.34 = (f32[24,24,128]{2,1,0:T(8,128)S(1)}, f32[24,24,128]{2,1,0:T(8,128)S(1)}, u32[]{:S(2)}, u32[]{:S(2)}) collective-permute-start(f32[24,24,128]{2,1,0:T(8,128)S(1)} %get-tuple-element.161), channel_id=1, source_target_pairs={{0,12},{2,14},{4,8},{6,10},{8,4},{10,6},{12,0},{14,2},{1,13},{3,15... | collective-permute-start | bytes 884744 | tf_op jit(solution)/shard_map/ppermute | solution.py:203
  94.0 36.9 %collective-permute-start.36 = (f32[24,24,128]{2,1,0:T(8,128)S(1)}, f32[24,24,128]{2,1,0:T(8,128)S(1)}, u32[]{:S(2)}, u32[]{:S(2)}) collective-permute-start(f32[24,24,128]{2,1,0:T(8,128)S(1)} %get-tuple-element.163), channel_id=1, source_target_pairs={{0,14},{2,12},{4,10},{6,8},{8,6},{10,4},{12,2},{14,0},{1,15},{3,13... | collective-permute-start | bytes 884744 | tf_op jit(solution)/shard_map/ppermute | solution.py:203
  97.6 36.6 %collective-permute-start.10 = (f32[24,24,128]{2,1,0:T(8,128)S(1)}, f32[24,24,128]{2,1,0:T(8,128)S(1)}, u32[]{:S(2)}, u32[]{:S(2)}) collective-permute-start(f32[24,24,128]{2,1,0:T(8,128)S(1)} %get-tuple-element.134), channel_id=1, source_target_pairs={{0,6},{2,4},{4,2},{6,0},{8,14},{10,12},{12,10},{14,8},{1,7},{3,5},... | collective-permute-start | bytes 884744 | tf_op jit(solution)/shard_map/ppermute | solution.py:203
  119.3 42.6 %collective-permute-start.13 = (f32[24,24,128]{2,1,0:T(8,128)S(1)}, f32[24,24,128]{2,1,0:T(8,128)S(1)}, u32[]{:S(2)}, u32[]{:S(2)}) collective-permute-start(f32[24,24,128]{2,1,0:T(8,128)S(1)} %get-tuple-element.137), channel_id=1, source_target_pairs={{0,8},{2,10},{4,12},{6,14},{8,0},{10,2},{12,4},{14,6},{1,9},{3,11}... | collective-permute-start | bytes 884744 | tf_op jit(solution)/shard_map/ppermute | solution.py:203
  119.3 49.9 %collective-permute-start.16 = (f32[24,24,128]{2,1,0:T(8,128)S(1)}, f32[24,24,128]{2,1,0:T(8,128)S(1)}, u32[]{:S(2)}, u32[]{:S(2)}) collective-permute-start(f32[24,24,128]{2,1,0:T(8,128)S(1)} %get-tuple-element.140), channel_id=1, source_target_pairs={{0,10},{2,8},{4,14},{6,12},{8,2},{10,0},{12,6},{14,4},{1,11},{3,9}... | collective-permute-start | bytes 884744 | tf_op jit(solution)/shard_map/ppermute | solution.py:203
  130.9 39.9 %collective-permute-start.19 = (f32[24,24,128]{2,1,0:T(8,128)S(1)}, f32[24,24,128]{2,1,0:T(8,128)S(1)}, u32[]{:S(2)}, u32[]{:S(2)}) collective-permute-start(f32[24,24,128]{2,1,0:T(8,128)S(1)} %get-tuple-element.143), channel_id=1, source_target_pairs={{0,12},{2,14},{4,8},{6,10},{8,4},{10,6},{12,0},{14,2},{1,13},{3,15... | collective-permute-start | bytes 884744 | tf_op jit(solution)/shard_map/ppermute | solution.py:203
  134.2 41.9 %collective-permute-start.22 = (f32[24,24,128]{2,1,0:T(8,128)S(1)}, f32[24,24,128]{2,1,0:T(8,128)S(1)}, u32[]{:S(2)}, u32[]{:S(2)}) collective-permute-start(f32[24,24,128]{2,1,0:T(8,128)S(1)} %get-tuple-element.146), channel_id=1, source_target_pairs={{0,14},{2,12},{4,10},{6,8},{8,6},{10,4},{12,2},{14,0},{1,15},{3,13... | collective-permute-start | bytes 884744 | tf_op jit(solution)/shard_map/ppermute | solution.py:203
  134.6 48.9 %collective-permute-start.4 = (f32[24,24,128]{2,1,0:T(8,128)S(1)}, f32[24,24,128]{2,1,0:T(8,128)S(1)}, u32[]{:S(2)}, u32[]{:S(2)}) collective-permute-start(f32[24,24,128]{2,1,0:T(8,128)S(1)} %get-tuple-element.128), channel_id=1, source_target_pairs={{0,2},{2,0},{4,6},{6,4},{8,10},{10,8},{12,14},{14,12},{1,3},{3,1},... | collective-permute-start | bytes 884744 | tf_op jit(solution)/shard_map/ppermute | solution.py:203
  161.9 41.5 %collective-permute-start.25 = (f32[32,24,128]{2,1,0:T(8,128)}, f32[32,24,128]{2,1,0:T(8,128)}, u32[]{:S(2)}, u32[]{:S(2)}) collective-permute-start(f32[32,24,128]{2,1,0:T(8,128)} %get-tuple-element.152), channel_id=1, source_target_pairs={{0,2},{2,0},{4,6},{6,4},{8,10},{10,8},{12,14},{14,12},{1,3},{3,1},... | collective-permute-start | bytes 1179656 | tf_op jit(solution)/shard_map/ppermute | solution.py:203
  169.2 36.9 %collective-permute-start.27 = (f32[32,24,128]{2,1,0:T(8,128)}, f32[32,24,128]{2,1,0:T(8,128)}, u32[]{:S(2)}, u32[]{:S(2)}) collective-permute-start(f32[32,24,128]{2,1,0:T(8,128)} %get-tuple-element.154), channel_id=1, source_target_pairs={{0,4},{2,6},{4,0},{6,2},{8,12},{10,14},{12,8},{14,10},{1,5},{3,7},... | collective-permute-start | bytes 1179656 | tf_op jit(solution)/shard_map/ppermute | solution.py:203
  170.7 36.8 %collective-permute-start.29 = (f32[32,24,128]{2,1,0:T(8,128)}, f32[32,24,128]{2,1,0:T(8,128)}, u32[]{:S(2)}, u32[]{:S(2)}) collective-permute-start(f32[32,24,128]{2,1,0:T(8,128)} %get-tuple-element.156), channel_id=1, source_target_pairs={{0,6},{2,4},{4,2},{6,0},{8,14},{10,12},{12,10},{14,8},{1,7},{3,5},... | collective-permute-start | bytes 1179656 | tf_op jit(solution)/shard_map/ppermute | solution.py:203
  176.1 31.4 %collective-permute-start.31 = (f32[32,24,128]{2,1,0:T(8,128)}, f32[32,24,128]{2,1,0:T(8,128)}, u32[]{:S(2)}, u32[]{:S(2)}) collective-permute-start(f32[32,24,128]{2,1,0:T(8,128)} %get-tuple-element.158), channel_id=1, source_target_pairs={{0,8},{2,10},{4,12},{6,14},{8,0},{10,2},{12,4},{14,6},{1,9},{3,11}... | collective-permute-start | bytes 1179656 | tf_op jit(solution)/shard_map/ppermute | solution.py:203
  200.6 62.0 %collective-permute-start.33 = (f32[32,24,128]{2,1,0:T(8,128)S(1)}, f32[32,24,128]{2,1,0:T(8,128)S(1)}, u32[]{:S(2)}, u32[]{:S(2)}) collective-permute-start(f32[32,24,128]{2,1,0:T(8,128)S(1)} %get-tuple-element.160), channel_id=1, source_target_pairs={{0,10},{2,8},{4,14},{6,12},{8,2},{10,0},{12,6},{14,4},{1,11},{3,9}... | collective-permute-start | bytes 1179656 | tf_op jit(solution)/shard_map/ppermute | solution.py:203
  203.4 59.2 %collective-permute-start.35 = (f32[32,24,128]{2,1,0:T(8,128)S(1)}, f32[32,24,128]{2,1,0:T(8,128)S(1)}, u32[]{:S(2)}, u32[]{:S(2)}) collective-permute-start(f32[32,24,128]{2,1,0:T(8,128)S(1)} %get-tuple-element.162), channel_id=1, source_target_pairs={{0,12},{2,14},{4,8},{6,10},{8,4},{10,6},{12,0},{14,2},{1,13},{3,15... | collective-permute-start | bytes 1179656 | tf_op jit(solution)/shard_map/ppermute | solution.py:203
  206.1 56.6 %collective-permute-start.37 = (f32[32,24,128]{2,1,0:T(8,128)S(1)}, f32[32,24,128]{2,1,0:T(8,128)S(1)}, u32[]{:S(2)}, u32[]{:S(2)}) collective-permute-start(f32[32,24,128]{2,1,0:T(8,128)S(1)} %get-tuple-element.164), channel_id=1, source_target_pairs={{0,14},{2,12},{4,10},{6,8},{8,6},{10,4},{12,2},{14,0},{1,15},{3,13... | collective-permute-start | bytes 1179656 | tf_op jit(solution)/shard_map/ppermute | solution.py:203
  207.5 59.7 %collective-permute-start.11 = (f32[32,24,128]{2,1,0:T(8,128)S(1)}, f32[32,24,128]{2,1,0:T(8,128)S(1)}, u32[]{:S(2)}, u32[]{:S(2)}) collective-permute-start(f32[32,24,128]{2,1,0:T(8,128)S(1)} %get-tuple-element.135), channel_id=1, source_target_pairs={{0,6},{2,4},{4,2},{6,0},{8,14},{10,12},{12,10},{14,8},{1,7},{3,5},... | collective-permute-start | bytes 1179656 | tf_op jit(solution)/shard_map/ppermute | solution.py:203
  207.5 88.7 %collective-permute-start.14 = (f32[32,24,128]{2,1,0:T(8,128)S(1)}, f32[32,24,128]{2,1,0:T(8,128)S(1)}, u32[]{:S(2)}, u32[]{:S(2)}) collective-permute-start(f32[32,24,128]{2,1,0:T(8,128)S(1)} %get-tuple-element.138), channel_id=1, source_target_pairs={{0,8},{2,10},{4,12},{6,14},{8,0},{10,2},{12,4},{14,6},{1,9},{3,11}... | collective-permute-start | bytes 1179656 | tf_op jit(solution)/shard_map/ppermute | solution.py:203
  262.6 59.2 %collective-permute-start.17 = (f32[32,24,128]{2,1,0:T(8,128)S(1)}, f32[32,24,128]{2,1,0:T(8,128)S(1)}, u32[]{:S(2)}, u32[]{:S(2)}) collective-permute-start(f32[32,24,128]{2,1,0:T(8,128)S(1)} %get-tuple-element.141), channel_id=1, source_target_pairs={{0,10},{2,8},{4,14},{6,12},{8,2},{10,0},{12,6},{14,4},{1,11},{3,9}... | collective-permute-start | bytes 1179656 | tf_op jit(solution)/shard_map/ppermute | solution.py:203
  262.6 59.2 %collective-permute-start.20 = (f32[32,24,128]{2,1,0:T(8,128)S(1)}, f32[32,24,128]{2,1,0:T(8,128)S(1)}, u32[]{:S(2)}, u32[]{:S(2)}) collective-permute-start(f32[32,24,128]{2,1,0:T(8,128)S(1)} %get-tuple-element.144), channel_id=1, source_target_pairs={{0,12},{2,14},{4,8},{6,10},{8,4},{10,6},{12,0},{14,2},{1,13},{3,15... | collective-permute-start | bytes 1179656 | tf_op jit(solution)/shard_map/ppermute | solution.py:203
  262.7 59.2 %collective-permute-start.23 = (f32[32,24,128]{2,1,0:T(8,128)S(1)}, f32[32,24,128]{2,1,0:T(8,128)S(1)}, u32[]{:S(2)}, u32[]{:S(2)}) collective-permute-start(f32[32,24,128]{2,1,0:T(8,128)S(1)} %get-tuple-element.147), channel_id=1, source_target_pairs={{0,14},{2,12},{4,10},{6,8},{8,6},{10,4},{12,2},{14,0},{1,15},{3,13... | collective-permute-start | bytes 1179656 | tf_op jit(solution)/shard_map/ppermute | solution.py:203
  267.3 54.6 %collective-permute-start.5 = (f32[32,24,128]{2,1,0:T(8,128)S(1)}, f32[32,24,128]{2,1,0:T(8,128)}, u32[]{:S(2)}, u32[]{:S(2)}) collective-permute-start(f32[32,24,128]{2,1,0:T(8,128)S(1)} %get-tuple-element.129), channel_id=1, source_target_pairs={{0,2},{2,0},{4,6},{6,4},{8,10},{10,8},{12,14},{14,12},{1,3},{3,1},... | collective-permute-start | bytes 1179656 | tf_op jit(solution)/shard_map/ppermute | solution.py:203
  296.2 25.7 %collective-permute-start.8 = (f32[32,24,128]{2,1,0:T(8,128)S(1)}, f32[32,24,128]{2,1,0:T(8,128)}, u32[]{:S(2)}, u32[]{:S(2)}) collective-permute-start(f32[32,24,128]{2,1,0:T(8,128)S(1)} %get-tuple-element.132), channel_id=1, source_target_pairs={{0,4},{2,6},{4,0},{6,2},{8,12},{10,14},{12,8},{14,10},{1,5},{3,7},... | collective-permute-start | bytes 1179656 | tf_op jit(solution)/shard_map/ppermute | solution.py:203
  351.3 25.5 %collective-permute-start.72 = (f32[24,24,128]{2,1,0:T(8,128)}, f32[24,24,128]{2,1,0:T(8,128)S(1)}, u32[]{:S(2)}, u32[]{:S(2)}) collective-permute-start(f32[24,24,128]{2,1,0:T(8,128)} %get-tuple-element.225), channel_id=1, source_target_pairs={{0,8},{2,10},{4,12},{6,14},{8,0},{10,2},{12,4},{14,6},{1,9},{3,11}... | collective-permute-start | bytes 884744 | tf_op jit(solution)/shard_map/ppermute | solution.py:203
  353.6 34.1 %collective-permute-start.73 = (f32[24,24,128]{2,1,0:T(8,128)}, f32[24,24,128]{2,1,0:T(8,128)S(1)}, u32[]{:S(2)}, u32[]{:S(2)}) collective-permute-start(f32[24,24,128]{2,1,0:T(8,128)} %get-tuple-element.226), channel_id=1, source_target_pairs={{0,10},{2,8},{4,14},{6,12},{8,2},{10,0},{12,6},{14,4},{1,11},{3,9}... | collective-permute-start | bytes 884744 | tf_op jit(solution)/shard_map/ppermute | solution.py:203
  357.0 32.7 %collective-permute-start.74 = (f32[24,24,128]{2,1,0:T(8,128)}, f32[24,24,128]{2,1,0:T(8,128)S(1)}, u32[]{:S(2)}, u32[]{:S(2)}) collective-permute-start(f32[24,24,128]{2,1,0:T(8,128)} %get-tuple-element.227), channel_id=1, source_target_pairs={{0,12},{2,14},{4,8},{6,10},{8,4},{10,6},{12,0},{14,2},{1,13},{3,15... | collective-permute-start | bytes 884744 | tf_op jit(solution)/shard_map/ppermute | solution.py:203
  366.7 51.7 %collective-permute-start.54 = (f32[48,24,128]{2,1,0:T(8,128)}, f32[48,24,128]{2,1,0:T(8,128)S(1)}, u32[]{:S(2)}, u32[]{:S(2)}) collective-permute-start(f32[48,24,128]{2,1,0:T(8,128)} %get-tuple-element.204), channel_id=1, source_target_pairs={{0,2},{2,0},{4,6},{6,4},{8,10},{10,8},{12,14},{14,12},{1,3},{3,1},... | collective-permute-start | bytes 1769480 | tf_op jit(solution)/shard_map/ppermute | solution.py:203
  372.3 54.8 %collective-permute-start.55 = (f32[48,24,128]{2,1,0:T(8,128)}, f32[48,24,128]{2,1,0:T(8,128)S(1)}, u32[]{:S(2)}, u32[]{:S(2)}) collective-permute-start(f32[48,24,128]{2,1,0:T(8,128)} %get-tuple-element.205), channel_id=1, source_target_pairs={{0,4},{2,6},{4,0},{6,2},{8,12},{10,14},{12,8},{14,10},{1,5},{3,7},... | collective-permute-start | bytes 1769480 | tf_op jit(solution)/shard_map/ppermute | solution.py:203
  377.6 27.9 %collective-permute-start.75 = (f32[24,24,128]{2,1,0:T(8,128)}, f32[24,24,128]{2,1,0:T(8,128)S(1)}, u32[]{:S(2)}, u32[]{:S(2)}) collective-permute-start(f32[24,24,128]{2,1,0:T(8,128)} %get-tuple-element.228), channel_id=1, source_target_pairs={{0,14},{2,12},{4,10},{6,8},{8,6},{10,4},{12,2},{14,0},{1,15},{3,13... | collective-permute-start | bytes 884744 | tf_op jit(solution)/shard_map/ppermute | solution.py:203
  390.4 27.3 %collective-permute-start.62 = (f32[24,24,128]{2,1,0:T(8,128)}, f32[24,24,128]{2,1,0:T(8,128)S(1)}, u32[]{:S(2)}, u32[]{:S(2)}) collective-permute-start(f32[24,24,128]{2,1,0:T(8,128)} %get-tuple-element.213), channel_id=1, source_target_pairs={{0,4},{2,6},{4,0},{6,2},{8,12},{10,14},{12,8},{14,10},{1,5},{3,7},... | collective-permute-start | bytes 884744 | tf_op jit(solution)/shard_map/ppermute | solution.py:203
  406.2 27.6 %collective-permute-start.56 = (f32[48,24,128]{2,1,0:T(8,128)}, f32[48,24,128]{2,1,0:T(8,128)S(1)}, u32[]{:S(2)}, u32[]{:S(2)}) collective-permute-start(f32[48,24,128]{2,1,0:T(8,128)} %get-tuple-element.206), channel_id=1, source_target_pairs={{0,6},{2,4},{4,2},{6,0},{8,14},{10,12},{12,10},{14,8},{1,7},{3,5},... | collective-permute-start | bytes 1769480 | tf_op jit(solution)/shard_map/ppermute | solution.py:203
  406.9 60.2 %collective-permute-start.57 = (f32[48,24,128]{2,1,0:T(8,128)}, f32[48,24,128]{2,1,0:T(8,128)S(1)}, u32[]{:S(2)}, u32[]{:S(2)}) collective-permute-start(f32[48,24,128]{2,1,0:T(8,128)} %get-tuple-element.207), channel_id=1, source_target_pairs={{0,8},{2,10},{4,12},{6,14},{8,0},{10,2},{12,4},{14,6},{1,9},{3,11}... | collective-permute-start | bytes 1769480 | tf_op jit(solution)/shard_map/ppermute | solution.py:203
  418.5 84.9 %collective-permute-start.58 = (f32[48,24,128]{2,1,0:T(8,128)}, f32[48,24,128]{2,1,0:T(8,128)}, u32[]{:S(2)}, u32[]{:S(2)}) collective-permute-start(f32[48,24,128]{2,1,0:T(8,128)} %get-tuple-element.208), channel_id=1, source_target_pairs={{0,10},{2,8},{4,14},{6,12},{8,2},{10,0},{12,6},{14,4},{1,11},{3,9}... | collective-permute-start | bytes 1769480 | tf_op jit(solution)/shard_map/ppermute | solution.py:203
  418.5 84.9 %collective-permute-start.59 = (f32[48,24,128]{2,1,0:T(8,128)}, f32[48,24,128]{2,1,0:T(8,128)}, u32[]{:S(2)}, u32[]{:S(2)}) collective-permute-start(f32[48,24,128]{2,1,0:T(8,128)} %get-tuple-element.209), channel_id=1, source_target_pairs={{0,12},{2,14},{4,8},{6,10},{8,4},{10,6},{12,0},{14,2},{1,13},{3,15... | collective-permute-start | bytes 1769480 | tf_op jit(solution)/shard_map/ppermute | solution.py:203
  427.1 76.2 %collective-permute-start.60 = (f32[48,24,128]{2,1,0:T(8,128)}, f32[48,24,128]{2,1,0:T(8,128)}, u32[]{:S(2)}, u32[]{:S(2)}) collective-permute-start(f32[48,24,128]{2,1,0:T(8,128)} %get-tuple-element.210), channel_id=1, source_target_pairs={{0,14},{2,12},{4,10},{6,8},{8,6},{10,4},{12,2},{14,0},{1,15},{3,13... | collective-permute-start | bytes 1769480 | tf_op jit(solution)/shard_map/ppermute | solution.py:203
  433.8 80.2 %collective-permute-start.63 = (f32[24,24,128]{2,1,0:T(8,128)}, f32[24,24,128]{2,1,0:T(8,128)S(1)}, u32[]{:S(2)}, u32[]{:S(2)}) collective-permute-start(f32[24,24,128]{2,1,0:T(8,128)} %get-tuple-element.214), channel_id=1, source_target_pairs={{0,6},{2,4},{4,2},{6,0},{8,14},{10,12},{12,10},{14,8},{1,7},{3,5},... | collective-permute-start | bytes 884744 | tf_op jit(solution)/shard_map/ppermute | solution.py:203
  467.2 72.8 %collective-permute-start.64 = (f32[24,24,128]{2,1,0:T(8,128)}, f32[24,24,128]{2,1,0:T(8,128)S(1)}, u32[]{:S(2)}, u32[]{:S(2)}) collective-permute-start(f32[24,24,128]{2,1,0:T(8,128)} %get-tuple-element.215), channel_id=1, source_target_pairs={{0,8},{2,10},{4,12},{6,14},{8,0},{10,2},{12,4},{14,6},{1,9},{3,11}... | collective-permute-start | bytes 884744 | tf_op jit(solution)/shard_map/ppermute | solution.py:203
  503.3 45.0 %collective-permute-start.65 = (f32[24,24,128]{2,1,0:T(8,128)}, f32[24,24,128]{2,1,0:T(8,128)S(1)}, u32[]{:S(2)}, u32[]{:S(2)}) collective-permute-start(f32[24,24,128]{2,1,0:T(8,128)} %get-tuple-element.216), channel_id=1, source_target_pairs={{0,10},{2,8},{4,14},{6,12},{8,2},{10,0},{12,6},{14,4},{1,11},{3,9}... | collective-permute-start | bytes 884744 | tf_op jit(solution)/shard_map/ppermute | solution.py:203
  503.3 45.0 %collective-permute-start.66 = (f32[24,24,128]{2,1,0:T(8,128)}, f32[24,24,128]{2,1,0:T(8,128)S(1)}, u32[]{:S(2)}, u32[]{:S(2)}) collective-permute-start(f32[24,24,128]{2,1,0:T(8,128)} %get-tuple-element.217), channel_id=1, source_target_pairs={{0,12},{2,14},{4,8},{6,10},{8,4},{10,6},{12,0},{14,2},{1,13},{3,15... | collective-permute-start | bytes 884744 | tf_op jit(solution)/shard_map/ppermute | solution.py:203
  503.4 45.0 %collective-permute-start.67 = (f32[24,24,128]{2,1,0:T(8,128)}, f32[24,24,128]{2,1,0:T(8,128)S(1)}, u32[]{:S(2)}, u32[]{:S(2)}) collective-permute-start(f32[24,24,128]{2,1,0:T(8,128)} %get-tuple-element.218), channel_id=1, source_target_pairs={{0,14},{2,12},{4,10},{6,8},{8,6},{10,4},{12,2},{14,0},{1,15},{3,13... | collective-permute-start | bytes 884744 | tf_op jit(solution)/shard_map/ppermute | solution.py:203
  514.1 133.1 %collective-permute-start.76 = (f32[24,192,128]{2,1,0:T(8,128)}, f32[24,192,128]{2,1,0:T(8,128)}, u32[]{:S(2)}, u32[]{:S(2)}) collective-permute-start(f32[24,192,128]{2,1,0:T(8,128)} %get-tuple-element.230), channel_id=1, source_target_pairs={{0,1},{1,0},{2,3},{3,2},{4,5},{5,4},{6,7},{7,6},{8,9},{9,8},{10,11... | collective-permute-start | bytes 7077896 | tf_op jit(solution)/shard_map/ppermute | solution.py:207
  556.0 99.1 %collective-permute-start.68 = (f32[24,192,128]{2,1,0:T(8,128)}, f32[24,192,128]{2,1,0:T(8,128)}, u32[]{:S(2)}, u32[]{:S(2)}) collective-permute-start(f32[24,192,128]{2,1,0:T(8,128)} %get-tuple-element.220), channel_id=1, source_target_pairs={{0,1},{1,0},{2,3},{3,2},{4,5},{5,4},{6,7},{7,6},{8,9},{9,8},{10,11... | collective-permute-start | bytes 7077896 | tf_op jit(solution)/shard_map/ppermute | solution.py:207
  566.7 27.4 %collective-permute-start.49 = (f32[8,48,128]{2,1,0:T(8,128)S(1)}, f32[8,48,128]{2,1,0:T(8,128)S(1)}, u32[]{:S(2)}, u32[]{:S(2)}) collective-permute-start(f32[8,48,128]{2,1,0:T(8,128)S(1)} %copy-done.75), channel_id=1, source_target_pairs={{0,8},{2,10},{4,12},{6,14},{8,0},{10,2},{12,4},{14,6},{1,9},{3,11}... | collective-permute-start | bytes 589832 | tf_op jit(solution)/shard_map/ppermute | solution.py:203
  609.3 28.6 %collective-permute-start.42 = (f32[8,48,128]{2,1,0:T(8,128)S(1)}, f32[8,48,128]{2,1,0:T(8,128)S(1)}, u32[]{:S(2)}, u32[]{:S(2)}) collective-permute-start(f32[8,48,128]{2,1,0:T(8,128)S(1)} %copy-done.78), channel_id=1, source_target_pairs={{0,10},{2,8},{4,14},{6,12},{8,2},{10,0},{12,6},{14,4},{1,11},{3,9}... | collective-permute-start | bytes 589832 | tf_op jit(solution)/shard_map/ppermute | solution.py:203
  (112 other events, 3285.7 us)
